TPU v7x, 128 devices: a whole 4x4x4 slice. The times are simulated.
128 devices in a mesh: wa: 16 (over x, z), ha: 8 (over y, core).
Axes of the slice: x: 4, y: 4, z: 4, core: 2. Of those that a mesh axis runs over, the one named last changes fastest.
Arguments:
- tokens: bfloat16 [512, 16384], P('ha', 'wa'), may hold values from -100 to 100, as said below
- norm_gain: float32 [16384], P('wa'), may hold values from 0.5 to 1.5
- gate_weight: bfloat16 [16384, 26624], P('wa', 'ha'), may hold values from -0.046875 to 0.046875
- up_weight: bfloat16 [16384, 26624], P('wa', 'ha'), may hold values from -0.046875 to 0.046875
- down_weight: bfloat16 [26624, 16384], P('ha', 'wa'), may hold values from -0.0390625 to 0.0390625
Outputs:
- mixed: bfloat16 [512, 16384], P('ha', 'wa')
Inputs may be any that keep to these rules, and one draw needn't show every extreme that they name: `tokens`: real-valued activations.
All inputs are finite; a program needn't handle non-finite values.
Results may differ from a plain program's by a relative error of at most 0.0064.
Values may be sent and summed in bfloat16 or wider, within the bound.
A program may use at most 128 MiB of HBM per device.

v0:
```python
import jax
import jax.numpy as jnp
from jax import lax
from jax.sharding import PartitionSpec as P


def activate(summed, hidden_width, model_width):
    gate = summed[:, :hidden_width]
    up = summed[:, hidden_width : 2 * hidden_width]
    squares = summed[:, 2 * hidden_width : 2 * hidden_width + 1]
    scale = lax.rsqrt(squares / model_width + 1e-05)
    return (jax.nn.silu(gate * scale) * (up * scale)).astype(jnp.bfloat16)


def body(tokens, norm_gain, gate_weight, up_weight, down_weight):
    gathered = lax.all_gather(tokens, "ha", axis=0, tiled=True)
    own_values = gathered.astype(jnp.float32)
    model_width = own_values.shape[1] * lax.axis_size("wa")
    squares = jnp.sum(own_values * own_values, axis=1, keepdims=True)
    scaled = (own_values * norm_gain[None, :]).astype(jnp.bfloat16)
    hidden_width = gate_weight.shape[1]
    gate_part = jnp.dot(scaled, gate_weight, preferred_element_type=jnp.float32)
    up_part = jnp.dot(scaled, up_weight, preferred_element_type=jnp.float32)
    square_block = jnp.broadcast_to(squares, (squares.shape[0], 128))
    summed = lax.psum_scatter(
        jnp.concatenate([gate_part, up_part, square_block], axis=1),
        "wa",
        scatter_dimension=0,
        tiled=True,
    )
    hidden = activate(summed, hidden_width, model_width)
    partial_out = jnp.dot(
        lax.all_gather(hidden, "wa", axis=0, tiled=True),
        down_weight,
        preferred_element_type=jnp.float32,
    )
    mixed_out = lax.psum_scatter(partial_out, "ha", scatter_dimension=0, tiled=True)
    return mixed_out.astype(jnp.bfloat16)


def solution(mesh):
    placed = (P("ha", "wa"), P("wa"), P("wa", "ha"), P("wa", "ha"), P("ha", "wa"))
    return jax.shard_map(body, mesh=mesh, in_specs=placed, out_specs=P("ha", "wa"), check_vma=False)
```

profile of v0, /device:TPU:0, one launch (start us, length us, event | category | flops | bytes accessed | tf_op | source)
XLA Modules:
  0.0 252.2 jit_solution(16157814636659487597)
XLA Ops:
  6.5 0.0 all-gather.3.cloned.1.call-start
  6.5 0.7 all-gather.3.cloned.1.call-update
  7.3 0.0 reduce-scatter.3.cloned.1.call-start
  7.3 27.6 %all-gather.3.cloned.1.call-done = bf16[512,1024]{1,0:T(8,128)(2,1)} async-done(((bf16[64,1024]{1,0:T(8,128)(2,1)}), bf16[512,1024]{1,0:T(8,128)(2,1)}) %all-gather.3.cloned.1.call-update) | async-done | bytes 1048592 | tf_op jit(solution)/shard_map/all_gather | solution.py:16
  34.9 0.0 slice-start
  34.9 1.7 fusion.1
  36.6 0.0 copy-start
  36.6 0.0 slice-start.1
  36.6 0.0 copy-start.1
  36.6 7.3 %fusion.2 = f32[512,3328]{1,0:T(8,128)S(1)} fusion(bf16[1024,3328]{1,0:T(8,128)(2,1)} %param.8, bf16[512,1024]{1,0:T(8,128)(2,1)} %all-gather.3.cloned.1.call-done, f32[1024]{0:T(1024)} %param.6), kind=kOutput, calls=%fused_computation.5 | convolution fusion | flops 3491233792 | bytes 14684160 | tf_op jit(solution)/shard_map/dot_general | solution.py:23
  43.9 0.0 slice-done
  43.9 0.0 copy-done
  43.9 0.0 slice-done.1
  43.9 0.0 copy-done.1
  44.0 3.7 %fusion.4 = f32[512,3328]{1,0:T(8,128)S(1)} fusion(bf16[1024,3328]{1,0:T(8,128)(2,1)S(1)} %bitcast.5, bf16[512,1024]{1,0:T(8,128)(2,1)S(1)} %copy-done, f32[1024]{0:T(1024)S(1)} %copy-done.1), kind=kOutput, calls=%fused_computation.6 | convolution fusion | flops 3491233792 | bytes 14684160 | tf_op jit(solution)/shard_map/dot_general | solution.py:22
  47.7 0.1 broadcast_in_dim.2
  47.8 5.3 %pad_maximum_fusion = f32[512,6784]{1,0:T(8,128)} fusion(f32[512,128]{1,0:T(8,128)S(1)} %broadcast_in_dim.2, f32[512,3328]{1,0:T(8,128)S(1)} %fusion.2, f32[512,3328]{1,0:T(8,128)S(1)} %fusion.4), kind=kLoop, calls=%fused_computation | loop fusion | flops 6946816 | bytes 27787264 | tf_op jit(solution)/shard_map/concatenate | solution.py:26
  53.1 0.0 reduce-scatter.3.cloned.1.call-update
  53.1 0.0 all-gather.5.cloned.1.call-start
  53.1 98.7 %reduce-scatter.3.cloned.1.call-done = f32[32,6784]{1,0:T(8,128)} async-done(((f32[512,6784]{1,0:T(8,128)}), f32[32,6784]{1,0:T(8,128)}) %reduce-scatter.3.cloned.1.call-update) | async-done | bytes 868368 | tf_op jit(solution)/shard_map/reduce_scatter | solution.py:25
  151.8 0.8 fusion.10
  152.6 2.0 fusion.7
  154.7 0.0 all-gather.5.cloned.1.call-update
  154.7 0.0 reduce-scatter.5.cloned.1.call-start
  154.7 47.7 %all-gather.5.cloned.1.call-done = bf16[512,3328]{1,0:T(8,128)(2,1)} async-done(((bf16[32,3328]{1,0:T(8,128)(2,1)}), bf16[512,3328]{1,0:T(8,128)(2,1)}) %all-gather.5.cloned.1.call-update) | async-done | bytes 3407888 | tf_op jit(solution)/shard_map/all_gather | solution.py:33
  202.4 9.0 %fusion.11 = f32[512,1024]{1,0:T(8,128)} fusion(bf16[512,3328]{1,0:T(8,128)(2,1)} %all-gather.5.cloned.1.call-done, bf16[3328,1024]{1,0:T(8,128)(2,1)} %param.9), kind=kOutput, calls=%fused_computation.15 | convolution fusion | flops 3489660928 | bytes 12320768 | tf_op jit(solution)/shard_map/dot_general | solution.py:32
  211.4 0.0 reduce-scatter.5.cloned.1.call-update
  211.5 32.6 %reduce-scatter.5.cloned.1.call-done = f32[64,1024]{1,0:T(8,128)} async-done(((f32[512,1024]{1,0:T(8,128)}), f32[64,1024]{1,0:T(8,128)}) %reduce-scatter.5.cloned.1.call-update) | async-done | bytes 262160 | tf_op jit(solution)/shard_map/reduce_scatter | solution.py:37
  244.0 1.6 convert_element_type.15
  (1 shorter events, 0.0 us)
Async XLA Ops:
  6.5 28.4 %all-gather.3.cloned.1.call-start = ((), (), s32[]{:S(2)}) async-start(), calls=%async_computation.2 | async-start | bytes 1179648 | tf_op jit(solution)/shard_map/all_gather | solution.py:16
  7.3 144.6 %reduce-scatter.3.cloned.1.call-start = ((), (), s32[]{:S(2)}) async-start(), calls=%async_computation.3 | async-start | bytes 14761984 | tf_op jit(solution)/shard_map/reduce_scatter | solution.py:25
  34.9 9.0 %slice-start = ((s8[6815744]{0:T(1024)(128)(4,1)}), s8[4194304]{0:T(1024)(128)(4,1)S(1)}, s32[]{:S(2)}) async-start(s8[6815744]{0:T(1024)(128)(4,1)} %bitcast.4), calls=%async_computation.6 | async-start | bytes 8388608
  36.6 7.3 %copy-start = (bf16[512,1024]{1,0:T(8,128)(2,1)S(1)}, bf16[512,1024]{1,0:T(8,128)(2,1)}, u32[]{:S(2)}) copy-start(bf16[512,1024]{1,0:T(8,128)(2,1)} %all-gather.3.cloned.1.call-done) | copy-start | bytes 3145732
  36.6 7.3 %slice-start.1 = ((s8[6815744]{0:T(1024)(128)(4,1)}), s8[2621440]{0:T(1024)(128)(4,1)S(1)}, s32[]{:S(2)}) async-start(s8[6815744]{0:T(1024)(128)(4,1)} %bitcast.4), calls=%async_computation.7 | async-start | bytes 5242880
  36.6 7.3 %copy-start.1 = (f32[1024]{0:T(1024)S(1)}, f32[1024]{0:T(1024)}, u32[]{:S(2)}) copy-start(f32[1024]{0:T(1024)} %param.6) | copy-start | bytes 12292
  53.1 149.3 %all-gather.5.cloned.1.call-start = ((), (), s32[]{:S(2)}) async-start(), calls=%async_computation.4 | async-start | bytes 3620864 | tf_op jit(solution)/shard_map/all_gather | solution.py:33
  154.7 89.3 %reduce-scatter.5.cloned.1.call-start = ((), (), s32[]{:S(2)}) async-start(), calls=%async_computation.5 | async-start | bytes 2359296 | tf_op jit(solution)/shard_map/reduce_scatter | solution.py:37
Sparse Core Ops, SparseCore 0:
  9.1 25.8 all-gather.2
  53.2 98.5 reduce-scatter.2
  154.8 47.5 all-gather.4
  211.6 32.3 reduce-scatter.4
where the time goes:
time: 252 us
  waiting for transfers between devices  207 us (82%)
  matrix products  20 us (8%)
  between operations  13.2 us (5%)
  other arithmetic  11.4 us (5%)
    reduce_scatter x1, waiting for transfers between devices, body(): lax.psum_scatter(jnp.concatenate([gate_part, up_part, square_block], axis...  98.7 us
    all_gather x1, waiting for transfers between devices, body(): lax.all_gather(hidden, 'wa', axis=0, tiled=True)  47.7 us
    reduce_scatter x1, waiting for transfers between devices, body(): lax.psum_scatter(partial_out, 'ha', scatter_dimension=0, tiled=True)  32.6 us
    all_gather x1, waiting for transfers between devices, body(): gathered = lax.all_gather(tokens, 'ha', axis=0, tiled=True)  27.6 us
    dot_general x1, matrix products, body(): jnp.dot(lax.all_gather(hidden, 'wa', axis=0, tiled=True), down_weight, pr...  9.01 us
    dot_general x1, matrix products, body(): up_part = jnp.dot(scaled, up_weight, preferred_element_type=jnp.float32)  7.28 us
    concatenate x1, other arithmetic, body(): jnp.concatenate([gate_part, up_part, square_block], axis=1)  5.25 us
  transfers between devices with their start and end apart: 4, of which 4 were waited for; matrix products, arithmetic and copies ran while one was open for 0% of the time, Pallas kernels for 0%

commit v1 on v0

--- a/solution.py
+++ b/solution.py
@@ -13,7 +13,11 @@
 
 
 def body(tokens, norm_gain, gate_weight, up_weight, down_weight):
-    gathered = lax.all_gather(tokens, "ha", axis=0, tiled=True)
+    n_lanes = lax.axis_size("ha")
+    cards = [n_lanes if p == 0 else 1 for p in range(tokens.ndim)]
+    gathered = lax.all_to_all(
+        jnp.tile(tokens, cards), "ha", split_axis=0, concat_axis=0, tiled=True
+    )
     own_values = gathered.astype(jnp.float32)
     model_width = own_values.shape[1] * lax.axis_size("wa")
     squares = jnp.sum(own_values * own_values, axis=1, keepdims=True)

time: 252 us -> 245 us (0.972)
  waiting for transfers between devices: 207 us -> 180 us
  blocking collectives: 0 us -> 20.5 us
    all_gather x1 -> x0, waiting for transfers between devices: 27.6 us -> none  [body(): gathered = lax.all_gather(tokens, 'ha', axis=0, tiled=True)]
    all_to_all x0 -> x1, blocking collectives: none -> 20.5 us  [body(): lax.all_to_all(jnp.tile(tokens, cards), 'ha', split_axis=0, concat_axis=0...]
  transfers between devices with their start and end apart: 4 -> 3, of which waited for: 4 -> 3; matrix products, arithmetic and copies ran while one was open for 0% -> 0% of each run, Pallas kernels for 0% -> 0%
where the time goes in v1:
time: 245 us
  waiting for transfers between devices  180 us (73%)
  blocking collectives  20.5 us (8%)
  matrix products  19 us (8%)
  between operations  13.2 us (5%)
  other arithmetic  11.1 us (5%)
    reduce_scatter x1, waiting for transfers between devices, body(): lax.psum_scatter(jnp.concatenate([gate_part, up_part, square_block], axis...  99.3 us
    all_gather x1, waiting for transfers between devices, body(): lax.all_gather(hidden, 'wa', axis=0, tiled=True)  47.7 us
    reduce_scatter x1, waiting for transfers between devices, body(): lax.psum_scatter(partial_out, 'ha', scatter_dimension=0, tiled=True)  32.6 us
    all_to_all x1, blocking collectives, body(): lax.all_to_all(jnp.tile(tokens, cards), 'ha', split_axis=0, concat_axis=0...  20.5 us
    dot_general x1, matrix products, body(): jnp.dot(lax.all_gather(hidden, 'wa', axis=0, tiled=True), down_weight, pr...  9.01 us
    dot_general x1, matrix products, body(): up_part = jnp.dot(scaled, up_weight, preferred_element_type=jnp.float32)  6.34 us
    concatenate x1, other arithmetic, body(): jnp.concatenate([gate_part, up_part, square_block], axis=1)  5.24 us
  transfers between devices with their start and end apart: 3, of which 3 were waited for; matrix products, arithmetic and copies ran while one was open for 0% of the time, Pallas kernels for 0%

profile of v1, /device:TPU:0, one launch (start us, length us, event | category | flops | bytes accessed | tf_op | source)
XLA Modules:
  0.0 244.6 jit_solution(1070338222243900285)
XLA Ops:
  6.5 0.0 reduce-scatter.3.cloned.1.call-start
  6.5 1.0 tile.2
  7.6 20.5 %all_to_all.6 = bf16[8,64,1024]{2,1,0:T(8,128)(2,1)S(1)} all-to-all(bf16[8,64,1024]{2,1,0:T(8,128)(2,1)S(1)} %tile.2), channel_id=1, replica_groups=mesh['wa'=16,'ha'=8] {'ha'}, dimensions={0} | all-to-all | bytes 2097152 | tf_op jit(solution)/shard_map/all_to_all | solution.py:18
  28.0 0.3 multiply_reduce_fusion
  28.3 0.1 broadcast_in_dim.4
  28.4 0.0 slice-start
  28.4 1.1 fusion
  29.4 0.0 slice-start.1
  29.5 6.3 %fusion.7 = f32[512,3328]{1,0:T(8,128)S(1)} fusion(bf16[512,1024]{1,0:T(8,128)(2,1)S(1)} %fusion, bf16[1024,3328]{1,0:T(8,128)(2,1)} %param.8), kind=kOutput, calls=%fused_computation.13 | convolution fusion | flops 3489660928 | bytes 14680064 | tf_op jit(solution)/shard_map/dot_general | solution.py:27
  35.8 0.0 slice-done
  35.8 0.0 slice-done.1
  35.8 3.7 %fusion.6 = f32[512,3328]{1,0:T(8,128)S(1)} fusion(bf16[512,1024]{1,0:T(8,128)(2,1)S(1)} %fusion, bf16[1024,3328]{1,0:T(8,128)(2,1)S(1)} %bitcast.11), kind=kOutput, calls=%fused_computation.12 | convolution fusion | flops 3489660928 | bytes 14680064 | tf_op jit(solution)/shard_map/dot_general | solution.py:26
  39.5 0.1 broadcast_in_dim.10
  39.7 5.2 %pad_maximum_fusion = f32[512,6784]{1,0:T(8,128)} fusion(f32[512,128]{1,0:T(8,128)S(1)} %broadcast_in_dim.10, f32[512,3328]{1,0:T(8,128)S(1)} %fusion.7, f32[512,3328]{1,0:T(8,128)S(1)} %fusion.6), kind=kLoop, calls=%fused_computation | loop fusion | flops 6946816 | bytes 27787264 | tf_op jit(solution)/shard_map/concatenate | solution.py:30
  44.9 0.0 reduce-scatter.3.cloned.1.call-update
  44.9 0.0 all-gather.2.cloned.1.call-start
  45.0 99.3 %reduce-scatter.3.cloned.1.call-done = f32[32,6784]{1,0:T(8,128)} async-done(((f32[512,6784]{1,0:T(8,128)}), f32[32,6784]{1,0:T(8,128)}) %reduce-scatter.3.cloned.1.call-update) | async-done | bytes 868368 | tf_op jit(solution)/shard_map/reduce_scatter | solution.py:29
  144.2 0.8 fusion.5
  145.1 2.0 fusion.2
  147.1 0.0 all-gather.2.cloned.1.call-update
  147.1 0.0 reduce-scatter.5.cloned.1.call-start
  147.2 47.7 %all-gather.2.cloned.1.call-done = bf16[512,3328]{1,0:T(8,128)(2,1)} async-done(((bf16[32,3328]{1,0:T(8,128)(2,1)}), bf16[512,3328]{1,0:T(8,128)(2,1)}) %all-gather.2.cloned.1.call-update) | async-done | bytes 3407888 | tf_op jit(solution)/shard_map/all_gather | solution.py:37
  194.9 9.0 %fusion.8 = f32[512,1024]{1,0:T(8,128)} fusion(bf16[512,3328]{1,0:T(8,128)(2,1)} %all-gather.2.cloned.1.call-done, bf16[3328,1024]{1,0:T(8,128)(2,1)} %param.9), kind=kOutput, calls=%fused_computation.14 | convolution fusion | flops 3489660928 | bytes 12320768 | tf_op jit(solution)/shard_map/dot_general | solution.py:36
  203.9 0.0 reduce-scatter.5.cloned.1.call-update
  203.9 32.6 %reduce-scatter.5.cloned.1.call-done = f32[64,1024]{1,0:T(8,128)} async-done(((f32[512,1024]{1,0:T(8,128)}), f32[64,1024]{1,0:T(8,128)}) %reduce-scatter.5.cloned.1.call-update) | async-done | bytes 262160 | tf_op jit(solution)/shard_map/reduce_scatter | solution.py:41
  236.5 1.6 convert_element_type.23
  (1 shorter events, 0.0 us)
Async XLA Ops:
  6.5 137.7 %reduce-scatter.3.cloned.1.call-start = ((), (), s32[]{:S(2)}) async-start(), calls=%async_computation.3 | async-start | bytes 14761984 | tf_op jit(solution)/shard_map/reduce_scatter | solution.py:29
  28.4 7.4 %slice-start = ((s8[6815744]{0:T(1024)(128)(4,1)}), s8[4194304]{0:T(1024)(128)(4,1)S(1)}, s32[]{:S(2)}) async-start(s8[6815744]{0:T(1024)(128)(4,1)} %bitcast.10), calls=%async_computation.6 | async-start | bytes 8388608
  29.4 6.4 %slice-start.1 = ((s8[6815744]{0:T(1024)(128)(4,1)}), s8[2621440]{0:T(1024)(128)(4,1)S(1)}, s32[]{:S(2)}) async-start(s8[6815744]{0:T(1024)(128)(4,1)} %bitcast.10), calls=%async_computation.7 | async-start | bytes 5242880
  44.9 150.0 %all-gather.2.cloned.1.call-start = ((), (), s32[]{:S(2)}) async-start(), calls=%async_computation.4 | async-start | bytes 3620864 | tf_op jit(solution)/shard_map/all_gather | solution.py:37
  147.1 89.4 %reduce-scatter.5.cloned.1.call-start = ((), (), s32[]{:S(2)}) async-start(), calls=%async_computation.5 | async-start | bytes 2359296 | tf_op jit(solution)/shard_map/reduce_scatter | solution.py:41
Sparse Core Ops, SparseCore 0:
  45.0 99.1 reduce-scatter.2
  147.2 47.5 all-gather.1
  204.0 32.3 reduce-scatter.4
